TPU v7x, 32 devices: a whole 2x2x4 slice. The times are simulated.
32 devices in a mesh: section: 2 (over x), dp: 16 (over z, y, core).
Axes of the slice: x: 2, y: 2, z: 4, core: 2. Of those that a mesh axis runs over, the one named last changes fastest.
Arguments:
- section_rows: bfloat16 [2, 2048, 1024], P('section', 'dp'), may hold values from -6 to 6
- lang_ids: int32 [2048], P('dp'), may hold values from 0 to 199, as said below
- lang_table: int32 [200], replicated, may hold values from 0 to 7, as said below
- lang_counts: int32 [16, 200], P('dp'), may hold values from 4 to 210
- temp_num: int32 [200], replicated, may hold values from 1 to 16
- weights: bfloat16 [2, 1024, 32768], P('section', None, 'dp'), may hold values from -0.1875 to 0.1875
Outputs:
- grads: float32 [2, 1024, 32768], P('section', None, 'dp')
- input_grad: bfloat16 [2048, 1024], P('dp', 'section')
Inputs may be any that keep to these rules, and one draw needn't show every extreme that they name: `lang_table`: every block is named by at least one language. `lang_ids`: on each replica (each aligned block of 128 rows) at most 32 rows map to any one block through lang_table, and one block receives exactly 32 rows from every replica.
All inputs are finite; a program needn't handle non-finite values.
Results may differ from a plain program's by a relative error of at most 0.0058.
Values may be sent and summed in bfloat16 or wider, within the bound.
No kernel may reach another device: no remote copies, remote signals or barrier semaphores. Data moves between devices by JAX's collectives and lax.ppermute only.
A program may use at most 64 MiB of HBM per device.

v0:
```python
import jax
import jax.numpy as jnp
from jax import lax
from jax.sharding import PartitionSpec as P


def partner(value, axis, bit):
    mask = 2**bit
    pairs = [(source, source ^ mask) for source in range(lax.axis_size(axis))]
    return lax.ppermute(value, axis, pairs)


def shifted(value, axis, steps):
    count = lax.axis_size(axis)
    first, last = (max(0, -steps), min(count, count - steps))
    return lax.ppermute(value, axis, [(source, source + steps) for source in range(first, last)])


def on_device(section_rows, lang_ids, lang_table, lang_counts, temp_num, weights):
    section_pos = lax.axis_index("section")
    replicas = lax.axis_size("dp")
    blocks_all = replicas // 2
    rows_dev = lang_ids.shape[0]
    capacity = 2 * rows_dev // blocks_all
    row_width = section_rows.shape[2]
    half_width = row_width // 2
    languages = lang_table.shape[0]
    own_weight = weights[0]
    lang_hot = lang_ids[:, None] == jnp.arange(languages, dtype=jnp.int32)[None, :]
    row_block = jnp.sum(jnp.where(lang_hot, lang_table[None, :], 0), axis=1)
    block_hot = (row_block[:, None] == jnp.arange(blocks_all, dtype=jnp.int32)[None, :]).astype(
        jnp.int32
    )
    running = jnp.cumsum(block_hot, axis=0) - 1
    slot_index = jnp.sum(running * block_hot, axis=1)
    target = row_block * capacity + slot_index
    placing = target[None, :] == jnp.arange(blocks_all * capacity, dtype=jnp.int32)[:, None]
    totals = lax.psum(lang_counts[0].astype(jnp.float32), "dp")
    lang_scale = 2.0 * replicas * temp_num.astype(jnp.float32) / totals
    row_scale = jnp.sum(jnp.where(lang_hot, lang_scale[None, :], 0.0), axis=1)
    local_rows = section_rows[0]
    weighted = (local_rows * row_scale[:, None]).astype(jnp.bfloat16)
    outgoing = jnp.where(section_pos == 1, weighted, local_rows)
    packed = jnp.dot(
        placing.astype(jnp.bfloat16), outgoing, preferred_element_type=jnp.float32
    ).astype(jnp.bfloat16)
    packed = packed.reshape(blocks_all, capacity, row_width)
    doubled = jnp.repeat(packed, 2, axis=0)
    arrived = lax.all_to_all(doubled, "dp", split_axis=0, concat_axis=0, tiled=True)
    projected = jnp.einsum("skd,df->skf", arrived, own_weight, preferred_element_type=jnp.float32)
    routed_flat = arrived.reshape(-1, row_width)
    projected = projected.reshape(routed_flat.shape[0], -1)
    handed = jnp.where(section_pos == 0, jnp.maximum(projected, 0.0), projected).astype(
        jnp.bfloat16
    )
    received = partner(handed, "section", 0)
    partner_term = jnp.where(
        (section_pos == 0) & (projected <= 0.0), jnp.zeros_like(received), received
    )
    weight_grad = lax.dot_general(
        routed_flat, partner_term, (((0,), (0,)), ((), ())), preferred_element_type=jnp.float32
    )

    def input_terms():
        return lax.dot_general(
            partner_term, own_weight, (((1,), (1,)), ((), ())), preferred_element_type=jnp.float32
        )

    def no_terms():
        return jnp.zeros((routed_flat.shape[0], row_width), jnp.float32)

    partial_rows = lax.cond(section_pos == 0, input_terms, no_terms)
    unplace = placing.astype(jnp.float32)
    came_back = lax.all_to_all(
        partial_rows.reshape(replicas, capacity, row_width),
        "dp",
        split_axis=0,
        concat_axis=0,
        tiled=True,
    )
    summed = (
        came_back.reshape(blocks_all, 2, capacity, row_width)
        .sum(axis=1)
        .reshape(blocks_all * capacity, row_width)
    )
    full_rows = lax.dot_general(
        unplace,
        summed,
        (((0,), (0,)), ((), ())),
        precision=lax.Precision.HIGHEST,
        preferred_element_type=jnp.float32,
    ).astype(jnp.bfloat16)
    right_cols = shifted(full_rows[:, half_width:], "section", 1)
    input_grad = jnp.where(section_pos == 0, full_rows[:, :half_width], right_cols)
    return (weight_grad[None], input_grad)


def solution(mesh):
    return jax.shard_map(
        on_device,
        mesh=mesh,
        in_specs=(
            P("section", "dp", None),
            P("dp"),
            P(),
            P("dp", None),
            P(),
            P("section", None, "dp"),
        ),
        out_specs=(P("section", None, "dp"), P("dp", "section")),
        check_vma=False,
    )
```

profile of v0, /device:TPU:1, one launch (start us, length us, event | category | flops | bytes accessed | tf_op | source)
XLA Modules:
  0.0 195.7 jit_solution(13366520089438789141)
XLA Ops:
  0.6 0.7 convert_element_type.35
  1.3 30.6 %psum.7 = f32[200]{0:T(256)S(1)} all-reduce(f32[200]{0:T(256)S(1)} %bitcast.31), channel_id=1, replica_groups=mesh['section'=2,'dp'=16] {'dp'}, use_global_device_ids=true, to_apply=%region_3.4 | all-reduce | flops 200 | bytes 1600 | tf_op jit(solution)/shard_map/psum | solution.py:38
  31.9 0.8 select_reduce_fusion.1
  32.7 0.7 multiply_divide_fusion
  33.3 0.8 select_reduce_fusion
  34.1 0.1 fusion.8
  34.2 0.2 reduce_window_sum.11
  34.4 0.2 select_reduce_fusion.2
  34.6 1.3 convolution_convert_fusion
  35.9 1.1 broadcast_in_dim.46
  37.0 7.8 %all-to-all-start = ((bf16[16,32,1024]{2,1,0:T(8,128)(2,1)}), bf16[16,32,1024]{2,1,0:T(8,128)(2,1)S(1)}, u32[]{:S(2)}, u32[]{:S(2)}) async-start(bf16[16,32,1024]{2,1,0:T(8,128)(2,1)} %bitcast.3), calls=%async_computation | async-start | bytes 2097152 | tf_op jit(solution)/shard_map/all_to_all | solution.py:49
  44.9 23.2 %all-to-all-done = bf16[16,32,1024]{2,1,0:T(8,128)(2,1)S(1)} async-done(((bf16[16,32,1024]{2,1,0:T(8,128)(2,1)}), bf16[16,32,1024]{2,1,0:T(8,128)(2,1)S(1)}, u32[]{:S(2)}, u32[]{:S(2)}) %all-to-all-start) | async-done | bytes 1048608 | tf_op jit(solution)/shard_map/all_to_all | solution.py:49
  68.0 7.3 %fusion = (bf16[512,2048]{1,0:T(8,128)(2,1)}, f32[512,2048]{1,0:T(8,128)}) fusion(pred[]{:T(512)S(6)} %eq.58, bf16[512,1024]{1,0:T(8,128)(2,1)S(1)} %bitcast.29, bf16[1,1024,2048]{2,1,0:T(8,128)(2,1)} %param.13), kind=kOutput, calls=%fused_computation.2 | convolution fusion | flops 2150629376 | bytes 11534337 | tf_op jit(solution)/shard_map/skd,df->skf/dot_general | solution.py:50
  75.3 1.2 collective-permute-start
  76.5 46.3 %collective-permute-done = bf16[512,2048]{1,0:T(8,128)(2,1)S(1)} collective-permute-done((bf16[512,2048]{1,0:T(8,128)(2,1)}, bf16[512,2048]{1,0:T(8,128)(2,1)S(1)}, u32[]{:S(2)}, u32[]{:S(2)}) %collective-permute-start) | collective-permute-done | bytes 2097184 | tf_op jit(solution)/shard_map/ppermute | solution.py:10
  122.9 4.5 %and_select_fusion = bf16[512,2048]{1,0:T(8,128)(2,1)} fusion(bf16[512,2048]{1,0:T(8,128)(2,1)S(1)} %collective-permute-done, f32[512,2048]{1,0:T(8,128)} %get-tuple-element.12, pred[]{:T(512)S(6)} %eq.58), kind=kLoop, calls=%fused_computation.3 | loop fusion | flops 3145728 | bytes 8388609 | tf_op jit(solution)/shard_map/jit(_where)/select_n | solution.py:57
  127.4 5.2 %conditional.1 = (f32[512,1024]{1,0:T(8,128)S(1)}) conditional(s32[]{:T(128)} %convert_element_type.40, () %tuple.14, (bf16[512,2048]{1,0:T(8,128)(2,1)}, bf16[1024,2048]{1,0:T(8,128)(2,1)}) %tuple.20), branch_computations={%region_5.6_spmd, %region_6.7_spmd} | conditional | flops 2147483648 | bytes 8388616 | solution.py:72
  127.4 5.2 %fusion.11 = f32[512,1024]{1,0:T(8,128)S(1)} fusion(bf16[512,2048]{1,0:T(8,128)(2,1)} %get-tuple-element.4, bf16[1024,2048]{1,0:T(8,128)(2,1)} %get-tuple-element.8), kind=kOutput, calls=%fused_computation.26 | convolution fusion | flops 2147483648 | bytes 8388608 | tf_op jit(solution)/shard_map/cond/branch_1_fun/dot_general | solution.py:65
  132.6 54.6 %all_to_all.10 = f32[16,32,1024]{2,1,0:T(8,128)S(1)} all-to-all(f32[16,32,1024]{2,1,0:T(8,128)S(1)} %bitcast.26), channel_id=1, replica_groups=mesh['section'=2,'dp'=16] {'dp'}, dimensions={0} | all-to-all | bytes 4194304 | tf_op jit(solution)/shard_map/all_to_all | solution.py:74
  187.2 0.0 copy-start
  187.2 0.2 bitcast_reduce_fusion
  187.4 0.5 convolution_convert_fusion.1
  187.9 1.3 collective-permute-start.1
  189.2 0.0 copy-done
  189.3 5.8 %convolution_bitcast_fusion = f32[1,1024,2048]{2,1,0:T(8,128)} fusion(bf16[512,1024]{1,0:T(8,128)(2,1)S(1)} %bitcast.30, bf16[512,2048]{1,0:T(8,128)(2,1)S(1)} %copy-done), kind=kOutput, calls=%fused_computation.1 | convolution fusion | flops 2147483648 | bytes 11534336 | tf_op jit(solution)/shard_map/dot_general | solution.py:60
  195.1 0.0 collective-permute-done.1
  195.1 0.7 slice_select_fusion
  (2 shorter events, 0.0 us)
Async XLA Ops:
  37.0 31.0 %all-to-all-start = ((bf16[16,32,1024]{2,1,0:T(8,128)(2,1)}), bf16[16,32,1024]{2,1,0:T(8,128)(2,1)S(1)}, u32[]{:S(2)}, u32[]{:S(2)}) async-start(bf16[16,32,1024]{2,1,0:T(8,128)(2,1)} %bitcast.3), calls=%async_computation | async-start | bytes 2097152 | tf_op jit(solution)/shard_map/all_to_all | solution.py:49
  75.3 47.6 %collective-permute-start = (bf16[512,2048]{1,0:T(8,128)(2,1)}, bf16[512,2048]{1,0:T(8,128)(2,1)S(1)}, u32[]{:S(2)}, u32[]{:S(2)}) collective-permute-start(bf16[512,2048]{1,0:T(8,128)(2,1)} %get-tuple-element.11), channel_id=1, source_target_pairs={{0,16},{16,0},{1,17},{17,1},{2,18},{18,2},{3,19},{19,3},{4,20},{20... | collective-permute-start | bytes 6291464 | tf_op jit(solution)/shard_map/ppermute | solution.py:10
  187.2 2.1 %copy-start = (bf16[512,2048]{1,0:T(8,128)(2,1)S(1)}, bf16[512,2048]{1,0:T(8,128)(2,1)}, u32[]{:S(2)}) copy-start(bf16[512,2048]{1,0:T(8,128)(2,1)} %and_select_fusion) | copy-start | bytes 6291460
  187.9 7.1 %collective-permute-start.1 = (bf16[128,512]{1,0:T(8,128)(2,1)S(1)}, bf16[128,512]{1,0:T(8,128)(2,1)S(1)}, u32[]{:S(2)}, u32[]{:S(2)}) collective-permute-start(bf16[128,512]{1,0:T(8,128)(2,1)S(1)} %slice.9), channel_id=1, source_target_pairs={{0,16},{1,17},{2,18},{3,19},{4,20},{5,21},{6,22},{7,23},{8,24},{9,... | collective-permute-start | bytes 393224 | tf_op jit(solution)/shard_map/ppermute | solution.py:16
where the time goes:
time: 196 us
  blocking collectives  85.2 us (43%)
  waiting for transfers between devices  69.5 us (35%)
  matrix products  20.1 us (10%)
  starting transfers between devices  10.4 us (5%)
  other arithmetic  8.72 us (4%)
    all_to_all x1, blocking collectives, on_device(): lax.all_to_all(partial_rows.reshape(replicas, capacity, row_width), 'dp',...  54.6 us
    ppermute x1, waiting for transfers between devices, partner(): return lax.ppermute(value, axis, pairs)  46.3 us
    psum x1, blocking collectives, on_device(): totals = lax.psum(lang_counts[0].astype(jnp.float32), 'dp')  30.6 us
    all_to_all x1, waiting for transfers between devices, on_device(): lax.all_to_all(doubled, 'dp', split_axis=0, concat_axis=0, tiled=True)  23.2 us
    all_to_all x1, starting transfers between devices, on_device(): lax.all_to_all(doubled, 'dp', split_axis=0, concat_axis=0, tiled=True)  7.84 us
    dot_general x1, matrix products, on_device(): jnp.einsum('skd,df->skf', arrived, own_weight, preferred_element_type=jnp...  7.29 us
    dot_general x1, matrix products, on_device(): lax.dot_general(routed_flat, partner_term, (((0,), (0,)), ((), ())), pref...  5.82 us
    dot_general x1, matrix products, input_terms(): lax.dot_general(partner_term, own_weight, (((1,), (1,)), ((), ())), prefe...  5.19 us
  transfers between devices with their start and end apart: 3, of which 2 were waited for; matrix products, arithmetic and copies ran while one was open for 3% of the time, Pallas kernels for 0%

commit v1 on v0

--- a/solution.py
+++ b/solution.py
@@ -35,7 +35,7 @@
     slot_index = jnp.sum(running * block_hot, axis=1)
     target = row_block * capacity + slot_index
     placing = target[None, :] == jnp.arange(blocks_all * capacity, dtype=jnp.int32)[:, None]
-    totals = lax.psum(lang_counts[0].astype(jnp.float32), "dp")
+    totals = jnp.sum(lax.all_gather(lang_counts[0].astype(jnp.float32), "dp"), axis=0)
     lang_scale = 2.0 * replicas * temp_num.astype(jnp.float32) / totals
     row_scale = jnp.sum(jnp.where(lang_hot, lang_scale[None, :], 0.0), axis=1)
     local_rows = section_rows[0]

time: 196 us -> 184 us (0.939)
  blocking collectives: 85.2 us -> 77.6 us
  starting transfers between devices: 10.4 us -> 6.14 us
    psum x1 -> x0, blocking collectives: 30.6 us -> none  [on_device(): totals = lax.psum(lang_counts[0].astype(jnp.float32), 'dp')]
    all_gather x0 -> x1, blocking collectives: none -> 23 us  [on_device(): lax.all_gather(lang_counts[0].astype(jnp.float32), 'dp')]
    all_to_all x1, starting transfers between devices: 7.84 us -> 3.63 us  [on_device(): lax.all_to_all(doubled, 'dp', split_axis=0, concat_axis=0, tiled=True)]
where the time goes in v1:
time: 184 us
  blocking collectives  77.6 us (42%)
  waiting for transfers between devices  69.5 us (38%)
  matrix products  20.1 us (11%)
  other arithmetic  8.76 us (5%)
  starting transfers between devices  6.14 us (3%)
    all_to_all x1, blocking collectives, on_device(): lax.all_to_all(partial_rows.reshape(replicas, capacity, row_width), 'dp',...  54.6 us
    ppermute x1, waiting for transfers between devices, partner(): return lax.ppermute(value, axis, pairs)  46.3 us
    all_to_all x1, waiting for transfers between devices, on_device(): lax.all_to_all(doubled, 'dp', split_axis=0, concat_axis=0, tiled=True)  23.2 us
    all_gather x1, blocking collectives, on_device(): lax.all_gather(lang_counts[0].astype(jnp.float32), 'dp')  23 us
    dot_general x1, matrix products, on_device(): jnp.einsum('skd,df->skf', arrived, own_weight, preferred_element_type=jnp...  7.29 us
    dot_general x1, matrix products, on_device(): lax.dot_general(routed_flat, partner_term, (((0,), (0,)), ((), ())), pref...  5.82 us
    dot_general x1, matrix products, input_terms(): lax.dot_general(partner_term, own_weight, (((1,), (1,)), ((), ())), prefe...  5.19 us
    select_n x1, other arithmetic, on_device(): jnp.where((section_pos == 0) & (projected <= 0.0), jnp.zeros_like(receive...  4.5 us
  transfers between devices with their start and end apart: 3, of which 2 were waited for; matrix products, arithmetic and copies ran while one was open for 3% of the time, Pallas kernels for 0%

profile of v1, /device:TPU:1, one launch (start us, length us, event | category | flops | bytes accessed | tf_op | source)
XLA Modules:
  0.0 184.0 jit_solution(11045727502593928971)
XLA Ops:
  0.6 0.7 convert_bitcast_fusion
  1.3 23.0 %all-gather = f32[16,1,200]{2,1,0:T(1,128)S(1)} all-gather(f32[1,1,200]{2,1,0:T(1,128)S(1)} %convert_bitcast_fusion), channel_id=1, replica_groups=mesh['section'=2,'dp'=16] {'dp'}, dimensions={0}, use_global_device_ids=true | all-gather | bytes 13600 | tf_op jit(solution)/shard_map/all_gather | solution.py:38
  24.3 0.8 select_reduce_fusion.1
  25.1 0.7 multiply_divide_fusion
  25.8 0.8 select_reduce_fusion
  26.5 0.1 fusion.8
  26.6 0.2 reduce_window_sum.11
  26.8 0.2 select_reduce_fusion.2
  27.0 1.3 convolution_convert_fusion
  28.3 1.1 broadcast_in_dim.46
  29.4 3.6 %all-to-all-start = ((bf16[16,32,1024]{2,1,0:T(8,128)(2,1)}), bf16[16,32,1024]{2,1,0:T(8,128)(2,1)S(1)}, u32[]{:S(2)}, u32[]{:S(2)}) async-start(bf16[16,32,1024]{2,1,0:T(8,128)(2,1)} %bitcast.3), calls=%async_computation | async-start | bytes 2097152 | tf_op jit(solution)/shard_map/all_to_all | solution.py:49
  33.1 23.2 %all-to-all-done = bf16[16,32,1024]{2,1,0:T(8,128)(2,1)S(1)} async-done(((bf16[16,32,1024]{2,1,0:T(8,128)(2,1)}), bf16[16,32,1024]{2,1,0:T(8,128)(2,1)S(1)}, u32[]{:S(2)}, u32[]{:S(2)}) %all-to-all-start) | async-done | bytes 1048608 | tf_op jit(solution)/shard_map/all_to_all | solution.py:49
  56.3 7.3 %fusion = (bf16[512,2048]{1,0:T(8,128)(2,1)}, f32[512,2048]{1,0:T(8,128)}) fusion(pred[]{:T(512)S(6)} %eq.58, bf16[512,1024]{1,0:T(8,128)(2,1)S(1)} %bitcast.30, bf16[1,1024,2048]{2,1,0:T(8,128)(2,1)} %param.13), kind=kOutput, calls=%fused_computation.2 | convolution fusion | flops 2150629376 | bytes 11534337 | tf_op jit(solution)/shard_map/skd,df->skf/dot_general | solution.py:50
  63.5 1.2 collective-permute-start
  64.8 46.3 %collective-permute-done = bf16[512,2048]{1,0:T(8,128)(2,1)S(1)} collective-permute-done((bf16[512,2048]{1,0:T(8,128)(2,1)}, bf16[512,2048]{1,0:T(8,128)(2,1)S(1)}, u32[]{:S(2)}, u32[]{:S(2)}) %collective-permute-start) | collective-permute-done | bytes 2097184 | tf_op jit(solution)/shard_map/ppermute | solution.py:10
  111.1 4.5 %and_select_fusion = bf16[512,2048]{1,0:T(8,128)(2,1)} fusion(bf16[512,2048]{1,0:T(8,128)(2,1)S(1)} %collective-permute-done, f32[512,2048]{1,0:T(8,128)} %get-tuple-element.12, pred[]{:T(512)S(6)} %eq.58), kind=kLoop, calls=%fused_computation.3 | loop fusion | flops 3145728 | bytes 8388609 | tf_op jit(solution)/shard_map/jit(_where)/select_n | solution.py:57
  115.6 5.2 %conditional.1 = (f32[512,1024]{1,0:T(8,128)S(1)}) conditional(s32[]{:T(128)} %convert_element_type.37, () %tuple.14, (bf16[512,2048]{1,0:T(8,128)(2,1)}, bf16[1024,2048]{1,0:T(8,128)(2,1)}) %tuple.20), branch_computations={%region_5.6_spmd, %region_6.7_spmd} | conditional | flops 2147483648 | bytes 8388616 | solution.py:72
  115.6 5.2 %fusion.11 = f32[512,1024]{1,0:T(8,128)S(1)} fusion(bf16[512,2048]{1,0:T(8,128)(2,1)} %get-tuple-element.4, bf16[1024,2048]{1,0:T(8,128)(2,1)} %get-tuple-element.8), kind=kOutput, calls=%fused_computation.27 | convolution fusion | flops 2147483648 | bytes 8388608 | tf_op jit(solution)/shard_map/cond/branch_1_fun/dot_general | solution.py:65
  120.8 54.6 %all_to_all.10 = f32[16,32,1024]{2,1,0:T(8,128)S(1)} all-to-all(f32[16,32,1024]{2,1,0:T(8,128)S(1)} %bitcast.27), channel_id=1, replica_groups=mesh['section'=2,'dp'=16] {'dp'}, dimensions={0} | all-to-all | bytes 4194304 | tf_op jit(solution)/shard_map/all_to_all | solution.py:74
  175.4 0.0 copy-start
  175.4 0.2 bitcast_reduce_fusion
  175.6 0.5 convolution_convert_fusion.1
  176.2 1.3 collective-permute-start.1
  177.5 0.0 copy-done
  177.5 5.8 %convolution_bitcast_fusion = f32[1,1024,2048]{2,1,0:T(8,128)} fusion(bf16[512,1024]{1,0:T(8,128)(2,1)S(1)} %bitcast.31, bf16[512,2048]{1,0:T(8,128)(2,1)S(1)} %copy-done), kind=kOutput, calls=%fused_computation.1 | convolution fusion | flops 2147483648 | bytes 11534336 | tf_op jit(solution)/shard_map/dot_general | solution.py:60
  183.3 0.0 collective-permute-done.1
  183.3 0.7 slice_select_fusion
  (3 shorter events, 0.1 us)
Async XLA Ops:
  29.4 26.8 %all-to-all-start = ((bf16[16,32,1024]{2,1,0:T(8,128)(2,1)}), bf16[16,32,1024]{2,1,0:T(8,128)(2,1)S(1)}, u32[]{:S(2)}, u32[]{:S(2)}) async-start(bf16[16,32,1024]{2,1,0:T(8,128)(2,1)} %bitcast.3), calls=%async_computation | async-start | bytes 2097152 | tf_op jit(solution)/shard_map/all_to_all | solution.py:49
  63.5 47.6 %collective-permute-start = (bf16[512,2048]{1,0:T(8,128)(2,1)}, bf16[512,2048]{1,0:T(8,128)(2,1)S(1)}, u32[]{:S(2)}, u32[]{:S(2)}) collective-permute-start(bf16[512,2048]{1,0:T(8,128)(2,1)} %get-tuple-element.11), channel_id=1, source_target_pairs={{0,16},{16,0},{1,17},{17,1},{2,18},{18,2},{3,19},{19,3},{4,20},{20... | collective-permute-start | bytes 6291464 | tf_op jit(solution)/shard_map/ppermute | solution.py:10
  175.4 2.1 %copy-start = (bf16[512,2048]{1,0:T(8,128)(2,1)S(1)}, bf16[512,2048]{1,0:T(8,128)(2,1)}, u32[]{:S(2)}) copy-start(bf16[512,2048]{1,0:T(8,128)(2,1)} %and_select_fusion) | copy-start | bytes 6291460
  176.2 7.1 %collective-permute-start.1 = (bf16[128,512]{1,0:T(8,128)(2,1)S(1)}, bf16[128,512]{1,0:T(8,128)(2,1)S(1)}, u32[]{:S(2)}, u32[]{:S(2)}) collective-permute-start(bf16[128,512]{1,0:T(8,128)(2,1)S(1)} %slice.9), channel_id=1, source_target_pairs={{0,16},{1,17},{2,18},{3,19},{4,20},{5,21},{6,22},{7,23},{8,24},{9,... | collective-permute-start | bytes 393224 | tf_op jit(solution)/shard_map/ppermute | solution.py:16
